TPU v7x, 512 devices: a whole 4x8x8 slice. The times are simulated.
512 devices in a mesh: flop: 4 (over x), turn: 16 (over y, core), river: 8 (over z).
Axes of the slice: x: 4, y: 8, z: 8, core: 2. Of those that a mesh axis runs over, the one named last changes fastest.
Arguments:
- regrets: float32 [4, 256, 1326], P('flop', ('turn', 'river')), may hold values from -6 to 6
- opp_reach: bfloat16 [4, 256, 1326], P('flop', ('turn', 'river')), may hold values from 0 to 1
- pot_size: int32 [4, 256], P('flop', ('turn', 'river')), may hold values from 1 to 8
- line_kind: int32 [4, 256], P('flop', ('turn', 'river')), may hold values from 0 to 2
- board_lines: int32 [4, 16, 16, 256], P('flop', 'turn', 'river'), may hold values from 0 to 255, as said below
- board_count: int32 [4, 16, 16], P('flop', 'turn', 'river'), may hold values from 64 to 256, as said below
- hand_ranks: int32 [4, 16, 16, 1326], P('flop', 'turn', 'river'), may hold values from 0 to 7461
- live_hands: int32 [4, 16, 16, 1326], P('flop', 'turn', 'river'), may hold values 0 or 1
Outputs:
- new_regrets: float32 [4, 256, 1326], P('flop', ('turn', 'river'))
- chance_values: float32 [128, 1326], P(('turn', 'river'))
Inputs may be any that keep to these rules, and one draw needn't show every extreme that they name: `board_lines`: each board lists 256 different lines of its flop; its first board_count slots hold the lines live on it, the other slots add nothing. `board_count`: in every flop one board has all 256 slots live and another only 64.
All inputs are finite; a program needn't handle non-finite values. No bound on the sum of `live_hands` on one device may be relied on, other than what follows from the above.
Results may differ from a plain program's by a relative error of at most 0.0003.
Values may be sent and summed in bfloat16 or wider, within the bound.
A program may use at most 64 MiB of HBM per device.

v0:
```python
import jax
import jax.numpy as jnp
import numpy as np
from jax import lax
from jax.sharding import PartitionSpec as P

CARDS = 52
ACTS = 2
floor_share = 0.1


def disjoint_table(card_count):
    card_first, card_second = np.triu_indices(card_count, 1)
    first_cards = jnp.asarray(card_first.astype(np.int32))
    second_cards = jnp.asarray(card_second.astype(np.int32))
    apart = (first_cards[:, None] != first_cards[None, :]) & (
        first_cards[:, None] != second_cards[None, :]
    )
    apart = (
        apart
        & (second_cards[:, None] != first_cards[None, :])
        & (second_cards[:, None] != second_cards[None, :])
    )
    return apart


def payoff_matrix(board_ranks, board_live, apart):
    both_live = apart & (board_live[:, None] > 0) & (board_live[None, :] > 0)
    fold_part = both_live.astype(jnp.float32)
    ordering = jnp.sign(board_ranks[None, :] - board_ranks[:, None]).astype(jnp.float32)
    return jnp.concatenate([fold_part * ordering, fold_part], axis=1).astype(jnp.bfloat16)


def on_device(
    regrets, opp_reach, pot_size, line_kind, board_lines, board_count, hand_ranks, live_hands
):
    hand_count = opp_reach.shape[2]
    boards_here = board_lines.shape[2]
    board_total = lax.axis_size("turn") * lax.axis_size("river") * boards_here
    pot_float = pot_size.astype(jnp.float32)
    show_coef = jnp.where(line_kind == 0, pot_float, 0.0)
    fold_coef = jnp.where(line_kind == 1, -pot_float, jnp.where(line_kind == 2, pot_float, 0.0))
    line_coef = jnp.stack([show_coef, fold_coef], axis=2).astype(jnp.bfloat16)
    reach_whole, coef_whole = (
        lax.all_gather(opp_reach, ("turn", "river"), axis=1, tiled=True),
        lax.all_gather(line_coef, ("turn", "river"), axis=1, tiled=True),
    )
    reach_whole = reach_whole[0]
    coef_whole = coef_whole[0]
    line_total = reach_whole.shape[0]
    slot_total = board_lines.shape[3]
    apart = disjoint_table(CARDS)
    chance_scale = 1.0 / (board_total * hand_count)
    line_table = jnp.zeros((line_total, hand_count), jnp.float32)
    for board_index in range(boards_here):
        slot_lines = board_lines[0, 0, board_index]
        live_count = board_count[0, 0, board_index]
        slot_reach = jnp.take(reach_whole, slot_lines, axis=0)
        slot_coef = jnp.take(coef_whole, slot_lines, axis=0).astype(jnp.float32)
        matrix = payoff_matrix(hand_ranks[0, 0, board_index], live_hands[0, 0, board_index], apart)

        def evaluate(
            first_row,
            row_count,
            slot_reach=slot_reach,
            slot_coef=slot_coef,
            matrix=matrix,
            live_count=live_count,
        ):
            products = jnp.dot(slot_reach, matrix, preferred_element_type=jnp.float32)
            slot_ids = first_row + jnp.arange(row_count, dtype=jnp.int32)
            keep_mask = (slot_ids < live_count).astype(jnp.float32)
            board_value = (
                slot_coef[:, 0:1] * products[:, :hand_count]
                + slot_coef[:, 1:2] * products[:, hand_count:]
            )
            return board_value * (chance_scale * keep_mask)[:, None]

        values = evaluate(0, slot_total)
        position = (
            jnp.full((line_total,), slot_total, jnp.int32)
            .at[slot_lines]
            .set(jnp.arange(slot_total, dtype=jnp.int32))
        )
        padded_values = jnp.concatenate([values, jnp.zeros((1, hand_count), jnp.float32)], axis=0)
        line_table = line_table + jnp.take(padded_values, position, axis=0)
    line_values = lax.psum_scatter(
        lax.slice_in_dim(
            line_table, 0, regrets.shape[1] * lax.axis_size(("turn", "river")), axis=0
        ),
        ("turn", "river"),
        scatter_dimension=0,
        tiled=True,
    )
    held_regret = regrets[0]
    group_total = held_regret.shape[0] // ACTS
    grouped = held_regret.reshape(group_total, ACTS, hand_count)
    worth_lines = line_values.reshape(group_total, ACTS, hand_count)
    positive = jnp.maximum(grouped, 0.0)
    strategy = (positive + floor_share) / (
        jnp.sum(positive, axis=1, keepdims=True) + ACTS * floor_share
    )
    node_values = jnp.sum(strategy * worth_lines, axis=1)
    updated = jnp.maximum(grouped + worth_lines - node_values[:, None, :], 0.0).reshape(
        held_regret.shape
    )
    chance_values = lax.psum(node_values, "flop") / lax.axis_size("flop")
    return (updated[None], chance_values)


def solution(mesh):
    placed = (
        P("flop", ("turn", "river"), None),
        P("flop", ("turn", "river"), None),
        P("flop", ("turn", "river")),
        P("flop", ("turn", "river")),
        P("flop", "turn", "river", None),
        P("flop", "turn", "river"),
        P("flop", "turn", "river", None),
        P("flop", "turn", "river", None),
    )
    return jax.shard_map(
        on_device,
        mesh=mesh,
        in_specs=placed,
        out_specs=(P("flop", ("turn", "river"), None), P(("turn", "river"), None)),
        check_vma=False,
    )
```

profile of v0, /device:TPU:24, one launch (start us, length us, event | category | flops | bytes accessed | tf_op | source)
XLA Modules:
  0.0 440.4 jit_solution(8097442302047093316)
XLA Ops:
  7.2 0.8 fusion.31
  8.0 0.8 compare_select_fusion.1
  8.8 0.7 copy.27
  9.5 94.9 %all_gather.7 = bf16[1,256,1326]{2,0,1:T(2,128)(2,1)S(1)} all-gather(bf16[1,2,1326]{2,0,1:T(2,128)(2,1)S(1)} %copy.27), channel_id=1, replica_groups=mesh['flop'=4,'turn'=16,'river'=8] {'turn','river'}, dimensions={1}, use_global_device_ids=true | all-gather | bytes 684216 | tf_op jit(solution)/shard_map/all_gather | solution.py:45
  104.7 67.3 %all_gather.6 = bf16[1,256,2]{2,0,1:T(2,128)(2,1)S(1)} all-gather(bf16[1,2,2]{2,0,1:T(2,128)(2,1)S(1)} %copy.24), channel_id=1, replica_groups=mesh['flop'=4,'turn'=16,'river'=8] {'turn','river'}, dimensions={1}, use_global_device_ids=true | all-gather | bytes 1032 | tf_op jit(solution)/shard_map/all_gather | solution.py:46
  172.2 1.3 gather_fusion.1
  173.6 0.9 gather_fusion
  174.5 2.1 gather_fusion.4
  176.6 0.9 gather_fusion.3
  177.5 1.4 scatter_custom_fusion
  178.9 1.4 scatter_custom_fusion.1
  180.8 0.6 fusion.32
  181.3 0.6 compare_select_fusion.7
  182.0 5.2 %convert_convert_fusion.1 = (bf16[1326,1326]{1,0:T(8,128)(2,1)S(1)}, bf16[1326,1326]{1,0:T(8,128)(2,1)}) fusion(pred[1326]{0:T(1024)(128)(4,1)S(1)} %get-tuple-element.11, s32[1326]{0:T(1024)S(1)} %copy-done.3, s32[1326]{0:T(1024)S(1)} %copy-done.2, pred[1326]{0:T(1024)(128)(4,1)S(1)} %get-tuple-element.12), kind=kLoop, calls=%fused_computation.10 | loop fusion | flops 26374140 | bytes 7046364 | tf_op jit(solution)/shard_map/convert.3
  187.2 8.7 %select_convert_fusion.1 = (bf16[1326,1326]{1,0:T(8,128)(2,1)S(1)}, bf16[1326,1326]{1,0:T(8,128)(2,1)}) fusion(s32[1326]{0:T(1024)S(1)} %get-tuple-element.9, pred[1326]{0:T(1024)(128)(4,1)S(1)} %get-tuple-element.11, s32[1326]{0:T(1024)S(1)} %copy-done.3, s32[1326]{0:T(1024)S(1)} %copy-done.2, s32[1326]{0:T(1024)S(1)} %get-tuple-element.10, ...), kind=kLoop, calls=%fused_computation.11 | loop fusion | flops 36923796 | bytes 7056972 | tf_op jit(solution)/shard_map/convert.2
  196.0 5.3 %fusion = f32[256,2652]{0,1:T(8,128)S(1)} fusion(bf16[1326,1326]{1,0:T(8,128)(2,1)S(1)} %get-tuple-element.15, bf16[1326,1326]{1,0:T(8,128)(2,1)S(1)} %get-tuple-element.13, bf16[256,1326]{1,0:T(8,128)(2,1)S(1)} %gather_fusion.1, pred[256]{0:T(512)(128)(4,1)S(1)} %compare_and_fusion.4), kind=kOutput, calls=%fused_computation.15 | convolution fusion | flops 1814880256 | bytes 10427920 | tf_op jit(solution)/shard_map/dot_general | solution.py:70
  201.3 0.3 fusion.11
  201.6 0.4 copy.36
  202.3 0.7 compare_select_fusion.6
  203.0 8.6 %fusion.4 = f32[256,2652]{0,1:T(8,128)S(1)} fusion(bf16[1326,1326]{1,0:T(8,128)(2,1)} %get-tuple-element.16, bf16[1326,1326]{1,0:T(8,128)(2,1)} %get-tuple-element.14, bf16[256,1326]{1,0:T(8,128)(2,1)} %gather_fusion.4, pred[256]{0:T(512)(128)(4,1)S(1)} %compare_and_fusion.2), kind=kOutput, calls=%fused_computation.19 | convolution fusion | flops 1814880256 | bytes 10427920 | tf_op jit(solution)/shard_map/dot_general | solution.py:70
  211.6 0.3 fusion.9
  211.8 1.6 copy.37
  213.5 1.3 copy-done.1
  214.9 2.3 gather_fusion.2
  217.2 2.3 gather_fusion.5
  219.5 2.7 select_add_fusion
  222.2 1.3 dynamic-slice
  224.2 196.0 %all-reduce.5.cloned.1.call-done = f32[256,1326]{1,0:T(8,128)} async-done(((f32[256,1326]{1,0:T(8,128)}), f32[256,1326]{1,0:T(8,128)}) %all-reduce.5.cloned.1.call-update) | async-done | bytes 1357840
  420.2 0.8 fusion.18
  421.1 10.5 %psum.7 = f32[1,1326]{1,0:T(1,128)S(1)} all-reduce(f32[1,1326]{1,0:T(1,128)S(1)} %reduce_sum.22), channel_id=1, replica_groups=mesh['flop'=4,'turn'=16,'river'=8] {'flop'}, use_global_device_ids=true, to_apply=%region_5.9 | all-reduce | flops 1326 | bytes 10608 | tf_op jit(solution)/shard_map/psum | solution.py:107
  431.6 0.6 broadcast_multiply_fusion
  432.2 1.4 subtract_maximum_fusion
  (51 shorter events, 1.5 us)
Async XLA Ops:
  7.2 97.4 %copy-start.9 = (s32[1,2]{1,0:T(1,128)S(1)}, s32[1,2]{1,0:T(1,128)}, u32[]{:S(2)}) copy-start(s32[1,2]{1,0:T(1,128)} %param.18) | copy-start | bytes 28
  7.2 97.4 %copy-start.8 = (s32[1,2]{1,0:T(1,128)S(1)}, s32[1,2]{1,0:T(1,128)}, u32[]{:S(2)}) copy-start(s32[1,2]{1,0:T(1,128)} %param.19) | copy-start | bytes 28
  7.2 413.1 %all-reduce.5.cloned.1.call-start = ((), (), s32[]{:S(2)}) async-start(), calls=%async_computation | async-start | bytes 2883584
  174.4 5.9 %copy-start.6 = (s32[1,1,2,1326]{3,2,1,0:T(2,128)S(1)}, s32[1,1,2,1326]{3,2,1,0:T(2,128)}, u32[]{:S(2)}) copy-start(s32[1,1,2,1326]{3,2,1,0:T(2,128)} %param.23) | copy-start | bytes 31828
  174.4 6.0 %copy-start.5 = (s32[1,1,2,1326]{3,2,1,0:T(2,128)S(1)}, s32[1,1,2,1326]{3,2,1,0:T(2,128)}, u32[]{:S(2)}) copy-start(s32[1,1,2,1326]{3,2,1,0:T(2,128)} %param.22) | copy-start | bytes 31828
  174.4 6.3 %copy-start.7 = (s32[1,1,2]{2,1,0:T(1,128)S(1)}, s32[1,1,2]{2,1,0:T(1,128)}, u32[]{:S(2)}) copy-start(s32[1,1,2]{2,1,0:T(1,128)} %param.21) | copy-start | bytes 28
  174.5 7.5 %copy-start.2 = (s32[1326]{0:T(1024)S(1)}, s32[1326]{0:T(1024)}, u32[]{:S(2)}) copy-start(s32[1326]{0:T(1024)} %constant.44.clone) | copy-start | bytes 15916
  174.5 7.5 %copy-start.3 = (s32[1326]{0:T(1024)S(1)}, s32[1326]{0:T(1024)}, u32[]{:S(2)}) copy-start(s32[1326]{0:T(1024)} %constant.45.clone) | copy-start | bytes 15916
  213.4 1.4 copy-start.1
  217.2 2.3 copy-start
  219.5 4.7 %copy-start.4 = (f32[1,2,1326]{2,1,0:T(2,128)S(1)}, f32[1,2,1326]{2,1,0:T(2,128)}, u32[]{:S(2)}) copy-start(f32[1,2,1326]{2,1,0:T(2,128)} %param.16) | copy-start | bytes 31828
Sparse Core Ops, SparseCore 0:
  222.3 197.8 all-reduce.4
where the time goes:
time: 441 us; the launch traced here: 440 us
  waiting for transfers between devices  196 us (44%)
  blocking collectives  173 us (39%)
  other arithmetic  22.5 us (5%)
  local copies, waits for them, and re-layouts  20.2 us (5%)
  between operations  15 us (3%)
  matrix products  13.9 us (3%)
    unnamed x2, waiting for transfers between devices  196 us
    all_gather x1, blocking collectives, on_device(): lax.all_gather(opp_reach, ('turn', 'river'), axis=1, tiled=True)  94.9 us
    all_gather x1, blocking collectives, on_device(): lax.all_gather(line_coef, ('turn', 'river'), axis=1, tiled=True)  67.3 us
    another operation x2, other arithmetic  14 us
    dot_general x2, matrix products, evaluate(): products = jnp.dot(slot_reach, matrix, preferred_element_type=jnp.float32)  13.9 us
    psum x1, blocking collectives, on_device(): chance_values = lax.psum(node_values, 'flop') / lax.axis_size('flop')  10.5 us
  transfers between devices with their start and end apart: 1, of which 1 were waited for; matrix products, arithmetic and copies ran while one was open for 0% of the time, Pallas kernels for 0%

commit v1 on v0

--- a/solution.py
+++ b/solution.py
@@ -7,6 +7,13 @@
 CARDS = 52
 ACTS = 2
 floor_share = 0.1
+
+
+def all_by_exchange(x, name, along):
+    size = lax.axis_size(name)
+    shards = jnp.stack([x for _ in range(size)])
+    shards = lax.all_to_all(shards, name, split_axis=0, concat_axis=0)
+    return jnp.concatenate(shards, axis=along)
 
 
 def disjoint_table(card_count):
@@ -43,7 +50,7 @@
     line_coef = jnp.stack([show_coef, fold_coef], axis=2).astype(jnp.bfloat16)
     reach_whole, coef_whole = (
         lax.all_gather(opp_reach, ("turn", "river"), axis=1, tiled=True),
-        lax.all_gather(line_coef, ("turn", "river"), axis=1, tiled=True),
+        all_by_exchange(line_coef, ("turn", "river"), 1),
     )
     reach_whole = reach_whole[0]
     coef_whole = coef_whole[0]

time: 441 us -> 391 us (0.89)
  blocking collectives: 173 us -> 99.1 us
  starting transfers between devices: 0.04 us -> 17.4 us
    all_gather x1 -> x0, blocking collectives: 67.3 us -> none  [on_device(): lax.all_gather(line_coef, ('turn', 'river'), axis=1, tiled=True)]
    all_to_all x0 -> x1, starting transfers between devices: none -> 17.3 us  [all_by_exchange(): shards = lax.all_to_all(shards, name, split_axis=0, concat_axis=0)]
    all_gather x1, blocking collectives: 94.9 us -> 88.6 us  [on_device(): lax.all_gather(opp_reach, ('turn', 'river'), axis=1, tiled=True)]
  transfers between devices with their start and end apart: 1 -> 2, of which waited for: 1 -> 1; matrix products, arithmetic and copies ran while one was open for 0% -> 10% of each run, Pallas kernels for 0% -> 0%
where the time goes in v1:
time: 391 us; the launch traced here: 390 us
  waiting for transfers between devices  198 us (51%)
  blocking collectives  99.1 us (25%)
  other arithmetic  26.2 us (7%)
  local copies, waits for them, and re-layouts  20.6 us (5%)
  starting transfers between devices  17.4 us (4%)
  between operations  15 us (4%)
  matrix products  13.5 us (3%)
    unnamed x2, waiting for transfers between devices  198 us
    all_gather x1, blocking collectives, on_device(): lax.all_gather(opp_reach, ('turn', 'river'), axis=1, tiled=True)  88.6 us
    all_to_all x1, starting transfers between devices, all_by_exchange(): shards = lax.all_to_all(shards, name, split_axis=0, concat_axis=0)  17.3 us
    dot_general x2, matrix products, evaluate(): products = jnp.dot(slot_reach, matrix, preferred_element_type=jnp.float32)  13.5 us
    another operation x2, other arithmetic  12.6 us
    psum x1, blocking collectives, on_device(): chance_values = lax.psum(node_values, 'flop') / lax.axis_size('flop')  10.5 us
  transfers between devices with their start and end apart: 2, of which 1 were waited for; matrix products, arithmetic and copies ran while one was open for 10% of the time, Pallas kernels for 0%

profile of v1, /device:TPU:24, one launch (start us, length us, event | category | flops | bytes accessed | tf_op | source)
XLA Modules:
  0.0 390.1 jit_solution(3814621316308221795)
XLA Ops:
  7.2 0.7 fusion.20
  8.0 0.7 stack.11
  8.6 17.3 %all-to-all-start = ((bf16[128,1,2,2]{3,2,1,0:T(2,128)(2,1)}), bf16[128,1,2,2]{3,2,1,0:T(2,128)(2,1)S(1)}, u32[]{:S(2)}, u32[]{:S(2)}) async-start(bf16[128,1,2,2]{3,2,1,0:T(2,128)(2,1)} %stack.11), calls=%async_computation | async-start | bytes 131072 | tf_op jit(solution)/shard_map/all_to_all | solution.py:15
  26.0 0.8 fusion.31
  26.8 0.8 compare_select_fusion.1
  27.6 1.4 scatter_custom_fusion
  29.0 1.4 scatter_custom_fusion.1
  30.5 0.8 compare_reduce_fusion.1
  31.3 0.8 slice_reduce_fusion.5
  32.1 0.7 copy.23
  32.8 88.6 %all_gather.3 = bf16[1,256,1326]{2,0,1:T(2,128)(2,1)S(1)} all-gather(bf16[1,2,1326]{2,0,1:T(2,128)(2,1)S(1)} %copy.23), channel_id=1, replica_groups=mesh['flop'=4,'turn'=16,'river'=8] {'turn','river'}, dimensions={1}, use_global_device_ids=true | all-gather | bytes 684216 | tf_op jit(solution)/shard_map/all_gather | solution.py:52
  122.1 0.6 compare_select_fusion.7
  122.8 1.3 gather_fusion.1
  124.1 1.3 gather_fusion.4
  125.5 4.4 %convert_convert_fusion.1 = (bf16[1326,1326]{1,0:T(8,128)(2,1)S(1)}, bf16[1326,1326]{1,0:T(8,128)(2,1)S(1)}) fusion(pred[1326]{0:T(1024)(128)(4,1)S(1)} %get-tuple-element.11, s32[1326]{0:T(1024)S(1)} %copy-done.3, s32[1326]{0:T(1024)S(1)} %copy-done.2, pred[1326]{0:T(1024)(128)(4,1)S(1)} %get-tuple-element.12), kind=kLoop, calls=%fused_computation.10 | loop fusion | flops 26374140 | bytes 7046364 | tf_op jit(solution)/shard_map/convert.3
  129.8 8.2 %select_convert_fusion.1 = (bf16[1326,1326]{1,0:T(8,128)(2,1)S(1)}, bf16[1326,1326]{1,0:T(8,128)(2,1)S(1)}) fusion(s32[1326]{0:T(1024)S(1)} %get-tuple-element.9, pred[1326]{0:T(1024)(128)(4,1)S(1)} %get-tuple-element.11, s32[1326]{0:T(1024)S(1)} %copy-done.3, s32[1326]{0:T(1024)S(1)} %copy-done.2, s32[1326]{0:T(1024)S(1)} %get-tuple-element.10, ...), kind=kLoop, calls=%fused_computation.11 | loop fusion | flops 36923796 | bytes 7056972 | tf_op jit(solution)/shard_map/convert.2
  138.1 6.8 %fusion = f32[256,2652]{0,1:T(8,128)} fusion(bf16[1326,1326]{1,0:T(8,128)(2,1)S(1)} %get-tuple-element.15, bf16[1326,1326]{1,0:T(8,128)(2,1)S(1)} %get-tuple-element.13, bf16[256,1326]{1,0:T(8,128)(2,1)S(1)} %gather_fusion.1, pred[256]{0:T(512)(128)(4,1)S(1)} %compare_and_fusion.4), kind=kOutput, calls=%fused_computation.15 | convolution fusion | flops 1814880256 | bytes 10427920 | tf_op jit(solution)/shard_map/dot_general | solution.py:77
  144.8 6.7 %fusion.4 = f32[256,2652]{0,1:T(8,128)} fusion(bf16[1326,1326]{1,0:T(8,128)(2,1)S(1)} %get-tuple-element.16, bf16[1326,1326]{1,0:T(8,128)(2,1)S(1)} %get-tuple-element.14, bf16[256,1326]{1,0:T(8,128)(2,1)S(1)} %gather_fusion.4, pred[256]{0:T(512)(128)(4,1)S(1)} %compare_and_fusion.2), kind=kOutput, calls=%fused_computation.19 | convolution fusion | flops 1814880256 | bytes 10427920 | tf_op jit(solution)/shard_map/dot_general | solution.py:77
  152.2 0.9 gather_fusion
  153.1 0.9 gather_fusion.3
  154.3 2.0 fusion.11
  157.0 2.2 fusion.9
  159.3 1.6 copy.32
  160.9 1.3 copy-done.1
  162.3 2.3 gather_fusion.2
  164.6 2.3 gather_fusion.5
  166.9 2.7 select_add_fusion
  169.7 1.3 dynamic-slice
  171.6 198.3 %all-reduce.5.cloned.1.call-done = f32[256,1326]{1,0:T(8,128)} async-done(((f32[256,1326]{1,0:T(8,128)}), f32[256,1326]{1,0:T(8,128)}) %all-reduce.5.cloned.1.call-update) | async-done | bytes 1357840
  369.9 0.8 fusion.18
  370.7 10.5 %psum.7 = f32[1,1326]{1,0:T(1,128)S(1)} all-reduce(f32[1,1326]{1,0:T(1,128)S(1)} %reduce_sum.22), channel_id=1, replica_groups=mesh['flop'=4,'turn'=16,'river'=8] {'flop'}, use_global_device_ids=true, to_apply=%region_5.9 | all-reduce | flops 1326 | bytes 10608 | tf_op jit(solution)/shard_map/psum | solution.py:114
  381.8 1.4 subtract_maximum_fusion
  (43 shorter events, 3.5 us)
Async XLA Ops:
  8.6 143.6 %all-to-all-start = ((bf16[128,1,2,2]{3,2,1,0:T(2,128)(2,1)}), bf16[128,1,2,2]{3,2,1,0:T(2,128)(2,1)S(1)}, u32[]{:S(2)}, u32[]{:S(2)}) async-start(bf16[128,1,2,2]{3,2,1,0:T(2,128)(2,1)} %stack.11), calls=%async_computation | async-start | bytes 131072 | tf_op jit(solution)/shard_map/all_to_all | solution.py:15
  26.0 95.5 %copy-start.5 = (s32[1,1,2]{2,1,0:T(1,128)S(1)}, s32[1,1,2]{2,1,0:T(1,128)}, u32[]{:S(2)}) copy-start(s32[1,1,2]{2,1,0:T(1,128)} %param.21) | copy-start | bytes 28
  26.0 343.9 %all-reduce.5.cloned.1.call-start = ((), (), s32[]{:S(2)}) async-start(), calls=%async_computation.1 | async-start | bytes 2883584
  124.1 1.3 copy-start.2
  124.1 1.3 copy-start.3
  160.8 1.4 copy-start.1
  164.6 2.3 copy-start
  166.9 4.7 %copy-start.4 = (f32[1,2,1326]{2,1,0:T(2,128)S(1)}, f32[1,2,1326]{2,1,0:T(2,128)}, u32[]{:S(2)}) copy-start(f32[1,2,1326]{2,1,0:T(2,128)} %param.16) | copy-start | bytes 31828
Sparse Core Ops, SparseCore 0:
  169.8 200.0 all-reduce.4
